TPU v7x, 128 devices: a whole 4x4x4 slice. The times are simulated.
128 devices in a mesh: grp: 4 (over x), vid: 32 (over y, z, core).
Axes of the slice: x: 4, y: 4, z: 4, core: 2. Of those that a mesh axis runs over, the one named last changes fastest.
Arguments:
- frames: bfloat16 [131072, 1024], P(('grp', 'vid')), parts along dimension 0, may hold values from -240 to 240
- w_frame: bfloat16 [1024, 512], replicated, may hold values from -0.1875 to 0.1875
- step_emb: bfloat16 [16384, 512], P(('grp', 'vid')), parts along dimension 0, may hold values from -6 to 6
- targets: int32 [131072], P(('grp', 'vid')), parts along dimension 0, may hold values from 0 to 127
- tile_frame: int32 [128, 128], P(('grp', 'vid')), parts along dimension 0, may hold values from 0 to 7, as said below
- tile_step: int32 [128, 128], P(('grp', 'vid')), parts along dimension 0, may hold values from 0 to 31, as said below
- tile_count: int32 [128], P(('grp', 'vid')), parts along dimension 0, may hold values from 8 to 128, as said below
Outputs:
- row_loss: float32 [131072], P(('grp', 'vid')), parts along dimension 0
- frame_grad: bfloat16 [131072, 1024], P(('grp', 'vid')), parts along dimension 0
- step_grad: float32 [16384, 512], P(('grp', 'vid')), parts along dimension 0
There are 4 independent parts, one for each index of `grp`. A program takes and returns all parts, laid end to end along the dimension named above; an argument that names none is the same for every part. Nothing has to cross between parts.
Inputs may be any that keep to these rules, and one draw needn't show every extreme that they name: `tile_frame`: each run of 8 tiles of a list, starting at a multiple of 8, names every frame block once. `tile_step`: the (frame block, step block) pairs of one video's list are distinct; the first 8 tiles pair each frame block with the video's own step block. Only the first tile_count tiles of a list are valid; some video's list is full.
All inputs are finite; a program needn't handle non-finite values.
Results may differ from a plain program's by a relative error of at most 0.0086.
Values may be sent and summed in bfloat16 or wider, within the bound.
A program may use at most 128 MiB of HBM per device.

v0:
```python
import math

import jax
import jax.numpy as jnp
from jax import lax
from jax.sharding import PartitionSpec as P


def shards(frames, w_frame, step_emb, targets, tile_frame, tile_step, tile_count):
    videos = lax.axis_size("vid")
    steps_own = step_emb.shape[0]
    width = step_emb.shape[1]
    frame_rows = frames.shape[0]
    temper = 1.0 / math.sqrt(width)
    blocks = frame_rows // 128
    embedded = jnp.dot(frames, w_frame, preferred_element_type=jnp.float32).astype(jnp.bfloat16)
    table = lax.all_gather(step_emb, "vid", axis=0, tiled=True)
    flat_table = table.reshape(videos, steps_own * width)
    frame_blocks = embedded.reshape(blocks, 128, width)
    rounds = tile_frame.shape[1] // blocks
    frame_tab = tile_frame.reshape(rounds, blocks)
    step_tab = tile_step.reshape(rounds, blocks)
    count = tile_count[0]
    block_ids = jnp.arange(blocks, dtype=jnp.int32)
    video_ids = jnp.arange(videos, dtype=jnp.int32)

    def round_scores(turn):
        frame_row = frame_tab[turn]
        step_row = step_tab[turn]
        slot_ok = (turn * blocks + block_ids < count).astype(jnp.int32)
        match = (frame_row[:, None] == block_ids[None, :]).astype(jnp.int32)
        step_for = jnp.sum(match * step_row[:, None], axis=0)
        valid = jnp.sum(match * slot_ok[:, None], axis=0) > 0
        picker = (step_for[:, None] == video_ids[None, :]).astype(jnp.bfloat16)
        cols = jnp.dot(picker, flat_table, preferred_element_type=jnp.float32).astype(jnp.bfloat16)
        cols = cols.reshape(blocks, steps_own, width)
        scores = (
            jnp.einsum("bre,bce->brc", frame_blocks, cols, preferred_element_type=jnp.float32)
            * temper
        )
        return (picker, valid, cols, scores)

    def forward_turn(carry, turn):
        best, total = carry
        picker, valid, cols, scores = round_scores(turn)
        tile_top = jnp.where(valid[:, None], jnp.max(scores, axis=2), -1e30)
        newest = jnp.maximum(best, tile_top)
        shifted = jnp.where(valid[:, None, None], scores - newest[:, :, None], -1e30)
        total = total * jnp.exp(best - newest) + jnp.sum(jnp.exp(shifted), axis=2)
        return ((newest, total), None)

    start_best = jnp.full((blocks, 128), -1e30, jnp.float32)
    start_total = jnp.zeros((blocks, 128), jnp.float32)
    (best, total), _ = lax.scan(
        forward_turn, (start_best, start_total), jnp.arange(rounds, dtype=jnp.int32)
    )
    lse = best + jnp.log(total)
    onehot = (targets[:, None] == jnp.arange(steps_own, dtype=jnp.int32)[None, :]).astype(
        jnp.bfloat16
    )
    chosen = jnp.dot(onehot, step_emb, preferred_element_type=jnp.float32)
    positive = jnp.sum(embedded.astype(jnp.float32) * chosen, axis=1) * temper
    row_loss = lse.reshape(-1) - positive

    def backward_turn(carry, turn):
        grad_frames, grad_steps = carry
        picker, valid, cols, scores = round_scores(turn)
        shifted = jnp.where(valid[:, None, None], scores - lse[:, :, None], -1e30)
        probs = jnp.exp(shifted).astype(jnp.bfloat16)
        toward_rows = (
            jnp.einsum("brc,bce->bre", probs, cols, preferred_element_type=jnp.float32) * temper
        )
        toward_cols = (
            jnp.einsum("brc,bre->bce", probs, frame_blocks, preferred_element_type=jnp.float32)
            * temper
        )
        added = lax.dot_general(
            picker.astype(jnp.float32),
            toward_cols.reshape(blocks, steps_own * width),
            (((0,), (0,)), ((), ())),
            precision=lax.Precision.HIGHEST,
            preferred_element_type=jnp.float32,
        )
        return ((grad_frames + toward_rows, grad_steps + added), None)

    start_frames = jnp.zeros((blocks, 128, width), jnp.float32)
    start_steps = jnp.zeros((videos, steps_own * width), jnp.float32)
    (grad_frames, grad_steps), _ = lax.scan(
        backward_turn, (start_frames, start_steps), jnp.arange(rounds, dtype=jnp.int32)
    )
    grad_rows = grad_frames.reshape(frame_rows, width) - chosen * temper
    frame_grad = lax.dot_general(
        grad_rows.astype(jnp.bfloat16),
        w_frame,
        (((1,), (1,)), ((), ())),
        preferred_element_type=jnp.float32,
    ).astype(jnp.bfloat16)
    flat_steps = grad_steps.reshape(videos * steps_own, width)
    returned = lax.psum_scatter(
        flat_steps.astype(jnp.bfloat16), "vid", scatter_dimension=0, tiled=True
    ).astype(jnp.float32)
    own_term = lax.dot_general(
        onehot, embedded, (((0,), (0,)), ((), ())), preferred_element_type=jnp.float32
    )
    step_grad = returned - own_term * temper
    return (row_loss, frame_grad, step_grad)


def solution(mesh):
    placed = (
        P(("grp", "vid"), None),
        P(),
        P(("grp", "vid"), None),
        P(("grp", "vid")),
        P(("grp", "vid"), None),
        P(("grp", "vid"), None),
        P(("grp", "vid")),
    )
    return jax.shard_map(
        shards,
        mesh=mesh,
        in_specs=placed,
        out_specs=(P(("grp", "vid")), P(("grp", "vid"), None), P(("grp", "vid"), None)),
        check_vma=False,
    )
```

profile of v0, /device:TPU:1, one launch (start us, length us, event | category | flops | bytes accessed | tf_op | source)
XLA Modules:
  0.0 623.4 jit_solution(14698518384547633666)
XLA Ops:
  20.3 40.1 %all-gather.2.cloned.1.call-done = bf16[4096,512]{1,0:T(8,128)(2,1)} async-done(((bf16[128,512]{1,0:T(8,128)(2,1)}), bf16[4096,512]{1,0:T(8,128)(2,1)}) %all-gather.2.cloned.1.call-update) | async-done | bytes 4194320 | tf_op jit(solution)/shard_map/all_gather | solution.py:17
  60.4 5.6 reshape.69
  66.0 123.6 %while.28 = (s32[]{:T(128)}, f32[8,128]{1,0:T(8,128)S(1)}, f32[8,128]{1,0:T(8,128)S(1)}, s32[16]{0:T(128)S(1)}, s32[16,8]{1,0:T(8,128)S(1)}, /*index=5*/s32[]{:T...) while((s32[]{:T(128)}, f32[8,128]{1,0:T(8,128)S(1)}, ...), condition=%wide.region_5.6_spmd.clone.clone, body=%wide.region_0.5_spmd.clone.clone.sunk | while | flops 168958560 | bytes 8442478 | solution.py:54
  190.2 333.3 %while.29 = (s32[]{:T(128)}, f32[8,128,512]{2,1,0:T(8,128)}, f32[32,65536]{1,0:T(8,128)}, s32[16]{0:T(128)S(1)}, s32[16,8]{1,0:T(8,128)S(1)}, /*index=5*/s32[]{:...) while((s32[]{:T(128)}, f32[8,128,512]{2,1,0:T(8,128)}, ...), condition=%wide.region_10.11_spmd.clone.clone, body=%wide.region_7.10_spmd.clone.clone.sunk | while | flops 644875072 | bytes 115086096 | solution.py:88
  201.9 5.8 convolution_add_fusion.2
  222.8 5.8 convolution_add_fusion.2
  243.6 5.8 convolution_add_fusion.2
  264.4 5.8 convolution_add_fusion.2
  285.3 5.8 convolution_add_fusion.2
  306.1 5.8 convolution_add_fusion.2
  326.9 5.8 convolution_add_fusion.2
  347.8 5.8 convolution_add_fusion.2
  368.6 5.8 convolution_add_fusion.2
  389.4 5.8 convolution_add_fusion.2
  410.3 5.8 convolution_add_fusion.2
  431.1 5.8 convolution_add_fusion.2
  451.9 5.8 convolution_add_fusion.2
  472.8 5.8 convolution_add_fusion.2
  493.6 5.8 convolution_add_fusion.2
  514.4 5.8 convolution_add_fusion.2
  523.5 5.8 convert_element_type.52
  529.3 5.6 convert_element_type.53
  537.9 5.1 convolution_convert_fusion.2
  543.0 71.4 %reduce-scatter.2.cloned.1.call-done = bf16[128,512]{1,0:T(8,128)(2,1)} async-done(((bf16[4096,512]{1,0:T(8,128)(2,1)}), bf16[128,512]{1,0:T(8,128)(2,1)}) %reduce-scatter.2.cloned.1.call-update) | async-done | bytes 131088 | tf_op jit(solution)/shard_map/reduce_scatter | solution.py:99
  (537 shorter events, 296.8 us)
Async XLA Ops:
  7.2 9.9 %copy-start = (bf16[1024,1024]{1,0:T(8,128)(2,1)S(1)}, bf16[1024,1024]{1,0:T(8,128)(2,1)}, u32[]{:S(2)}) copy-start(bf16[1024,1024]{1,0:T(8,128)(2,1)} %param.11) | copy-start | bytes 6291460
  7.2 53.2 %all-gather.2.cloned.1.call-start = ((), (), s32[]{:S(2)}) async-start(), calls=%async_computation.1 | async-start | bytes 4325376 | tf_op jit(solution)/shard_map/all_gather | solution.py:17
  7.9 606.4 %reduce-scatter.2.cloned.1.call-start = ((), (), s32[]{:S(2)}) async-start(), calls=%async_computation.2 | async-start | bytes 4325376 | tf_op jit(solution)/shard_map/reduce_scatter | solution.py:99
  197.0 4.4 slice-start
  198.6 3.3 slice-start.1
  217.9 4.4 slice-start
  219.5 3.3 slice-start.1
  238.7 4.4 slice-start
  240.3 3.3 slice-start.1
  259.5 4.4 slice-start
  280.4 4.4 slice-start
  301.2 4.4 slice-start
  322.0 4.4 slice-start
  342.9 4.4 slice-start
  363.7 4.4 slice-start
  384.5 4.4 slice-start
  386.1 3.3 slice-start.1
  405.4 4.4 slice-start
  426.2 4.4 slice-start
  447.0 4.4 slice-start
  467.9 4.4 slice-start
  488.7 4.4 slice-start
  509.5 4.4 slice-start
  537.9 76.5 %copy-start.4 = (s32[1024]{0:T(1024)S(1)}, s32[1024]{0:T(1024)}, u32[]{:S(2)}) copy-start(s32[1024]{0:T(1024)} %param.14) | copy-start | bytes 12292
  (60 other events, 143.7 us)
Sparse Core Ops, SparseCore 0:
  10.3 50.0 all-gather.1
  535.0 79.2 reduce-scatter.1
where the time goes:
time: 628 us; the launch traced here: 623 us
  matrix products  243 us (39%)
  local copies, waits for them, and re-layouts  131 us (21%)
  waiting for transfers between devices  112 us (18%)
  loops' own time  85.7 us (14%)
  other arithmetic  37.1 us (6%)
  between operations  14.1 us (2%)
    while x192, local copies, waits for them, and re-layouts  94.2 us
    dot_general x16, matrix products, backward_turn(): lax.dot_general(picker.astype(jnp.float32), toward_cols.reshape(blocks, s...  93.2 us
    dot_general x32, matrix products, round_scores(): jnp.dot(picker, flat_table, preferred_element_type=jnp.float32)  92.9 us
    reduce_scatter x1, waiting for transfers between devices, shards(): lax.psum_scatter(flat_steps.astype(jnp.bfloat16), 'vid', scatter_dimensio...  71.4 us
    another operation x1, loops' own time, shards(): lax.scan(backward_turn, (start_frames, start_steps), jnp.arange(rounds, d...  43.3 us
    another operation x1, loops' own time, shards(): lax.scan(forward_turn, (start_best, start_total), jnp.arange(rounds, dtyp...  42.4 us
    all_gather x1, waiting for transfers between devices, shards(): table = lax.all_gather(step_emb, 'vid', axis=0, tiled=True)  40.1 us
    convert_element_type x32, other arithmetic, round_scores(): slot_ok = (turn * blocks + block_ids < count).astype(jnp.int32)  20.8 us
  transfers between devices with their start and end apart: 2, of which 2 were waited for; matrix products, arithmetic and copies ran while one was open for 3% of the time, Pallas kernels for 0%

commit v1 on v0

v1 whole, which is shorter than its diff:
```python
import functools
import math

import jax
import jax.numpy as jnp
from jax import lax
from jax.experimental import pallas as pl
from jax.experimental.pallas import tpu as pltpu
from jax.sharding import PartitionSpec as P

F32 = jnp.float32
BF16 = jnp.bfloat16
MESH = pl.DeviceIdType.MESH
NT = (((1,), (1,)), ((), ()))
SIDE = 4
CHIPS = SIDE * SIDE
BLK = 128
LOG2E = 1.0 / math.log(2.0)
LN2 = math.log(2.0)
FAR = -1e30

ORDER = [
    (0, 0), (0, 1), (1, 0), (0, 3), (3, 0), (1, 1), (3, 3), (1, 3),
    (3, 1), (2, 0), (0, 2), (2, 1), (1, 2), (2, 3), (3, 2), (2, 2),
]
POS = {place: k for k, place in enumerate(ORDER)}
TURN = [POS[(db, da)] for da, db in ORDER]

GATHER = {
    0: [(3, 0), (1, 0), (0, 3), (0, 1)],
    3: [(2, 0), (3, 3), (1, 1), (3, 1), (1, 3), (0, 2)],
    10: [(2, 1), (2, 3), (1, 2), (3, 2)],
    14: [(2, 2)],
}
ONWARD = {
    (0, 0): ["a+", "a-", "b+", "b-"],
    (3, 0): ["a+", "b+", "b-"],
    (1, 0): ["b+", "b-"],
    (2, 0): ["b+", "b-"],
    (0, 3): ["b+"],
    (1, 3): ["b+"],
    (2, 1): ["b-"],
    (3, 1): ["b-"],
}
SHIFT = {"a+": (-1, 0), "a-": (1, 0), "b+": (0, -1), "b-": (0, 1)}

LANDS = ["h0", "h1", "h2", "h3", "p0", "p1", "p2", "p3",
         "m0", "m1", "m2", "m3", "A", "Ap", "Am"]
LAND = {name: i for i, name in enumerate(LANDS)}
COMBINE = {
    (2, 2): ([], "b-", "h2"),
    (3, 2): ([], "b-", "h3"),
    (1, 2): ([], "b+", "h1"),
    (0, 2): ([], "b+", "h0"),
    (2, 3): (["h2"], "b-", "m2"),
    (3, 3): (["h3"], "b-", "m3"),
    (1, 3): ([], "b-", "m1"),
    (0, 3): ([], "b-", "m0"),
    (2, 1): ([], "b+", "p2"),
    (3, 1): ([], "b+", "p3"),
    (1, 1): (["h1"], "b+", "p1"),
    (0, 1): (["h0"], "b+", "p0"),
    (2, 0): (["p2", "m2"], "a+", "A"),
    (1, 0): (["p1", "m1", "A"], "a+", "Ap"),
    (3, 0): (["p3", "m3"], "a-", "Am"),
}
REDUCE = {
    1: [(2, 2)],
    3: [(3, 2)],
    4: [(2, 3)],
    5: [(2, 1), (1, 2)],
    7: [(0, 2)],
    8: [(2, 0)],
    9: [(1, 3), (3, 1)],
    10: [(3, 3)],
    11: [(1, 1)],
    13: [(3, 0), (0, 3)],
    14: [(0, 1)],
    15: [(1, 0)],
}


def kernel(
    step_in, tgt, tile_frame, tile_step, count, frames_hbm, w_hbm,
    loss, grad_hbm, step_grad,
    frames, w, emb, table, table_t, scores, probs, bias, top, total, shift,
    onehot, own, part, side_tx, side_rx, tx, rx, grad,
    load_sem, ag_send, ag_mine, ag_other, rs_send, rs_recv, side_send, side_recv,
    store_sem,
):
    n_frames, width = emb.shape
    blocks = n_frames // BLK
    cols = 256
    pieces = n_frames // cols
    temper = 1.0 / math.sqrt(width)

    me = lax.axis_index("vid")
    core = me % 2
    z = (me // 2) % SIDE
    y = me // (2 * SIDE)

    def owner(da, db, other):
        ya = (y + da * (1 - core) + db * core) % SIDE
        zb = (z + db * (1 - core) + da * core) % SIDE
        kind = core + other * (1 - 2 * core)
        return (ya * SIDE + zb) * 2 + kind

    dev = {
        "a+": owner(1, 0, 0), "a-": owner(3, 0, 0),
        "b+": owner(0, 1, 0), "b-": owner(0, 3, 0),
        "side": owner(0, 0, 1),
    }

    load_frames = pltpu.make_async_copy(frames_hbm, frames, load_sem.at[0])
    load_w = pltpu.make_async_copy(w_hbm, w, load_sem.at[1])
    load_frames.start()
    load_w.start()

    barrier = pltpu.get_barrier_semaphore()
    for name in dev:
        pl.semaphore_signal(barrier, inc=1, device_id={"vid": dev[name]}, device_id_type=MESH)
    table[0, 0:BLK, :] = step_in[...]
    pl.semaphore_wait(barrier, len(dev))

    def mine(k):
        return table.at[k, pl.ds(0, BLK)]

    def others(k):
        return table.at[k, pl.ds(BLK, BLK)]

    def remote(src, dst, send, recv, name):
        return pltpu.make_async_remote_copy(
            src_ref=src, dst_ref=dst, send_sem=send, recv_sem=recv,
            device_id={"vid": dev[name]}, device_id_type=MESH,
        )

    sends = []

    def pass_on(place):
        k = POS[place]
        for name in ONWARD.get(place, []):
            sa, sb = SHIFT[name]
            land = POS[((place[0] + sa) % SIDE, (place[1] + sb) % SIDE)]
            sends.append(k)
            remote(mine(k), mine(land), ag_send.at[len(sends) - 1], ag_mine.at[land], name).start()
        sends.append(k)
        remote(
            mine(k), others(TURN[k]), ag_send.at[len(sends) - 1], ag_other.at[TURN[k]], "side"
        ).start()

    def arrive(place):
        k = POS[place]
        remote(mine(k), mine(k), ag_send.at[0], ag_mine.at[k], "side").wait_recv()
        pass_on(place)

    pass_on((0, 0))

    row = lax.broadcasted_iota(jnp.int32, (2 * CHIPS, BLK), 0)
    ids = jnp.zeros((2 * CHIPS, BLK), jnp.int32)
    for k, (da, db) in enumerate(ORDER):
        for other in range(2):
            ids = jnp.where(row == 2 * k + other, owner(da, db, other), ids)
    step_hot = jnp.where(ids == tile_step[...], 1.0, 0.0).astype(BF16)
    block_of = lax.broadcasted_iota(jnp.int32, (n_frames, BLK), 0) // BLK
    slot = lax.broadcasted_iota(jnp.int32, (n_frames, BLK), 1)
    frame_hot = jnp.where(
        (block_of == tile_frame[...]) & (slot < count[0]), 1.0, 0.0
    ).astype(BF16)
    seen = lax.dot_general(step_hot, frame_hot, NT, preferred_element_type=F32)
    hidden = jnp.where(seen > 0.5, 0.0, FAR)
    for k in range(CHIPS):
        bias[k] = hidden[2 * k : 2 * k + 2, :]
    label = lax.broadcasted_iota(jnp.int32, (BLK, BLK), 0)
    for b in range(blocks):
        onehot[:, b * BLK : (b + 1) * BLK] = jnp.where(
            label == tgt[b : b + 1, :], 1.0, 0.0
        ).astype(BF16)
    top[...] = jnp.full_like(top, FAR)
    total[...] = jnp.zeros_like(total)

    load_frames.wait()
    load_w.wait()
    for n in range(pieces):
        rows = slice(n * cols, (n + 1) * cols)
        emb[rows, :] = jnp.dot(
            frames[rows, :], w[...], preferred_element_type=F32
        ).astype(BF16)

    @pl.loop(0, CHIPS)
    def _(k):
        for step in GATHER:
            @pl.when(k == step)
            def _():
                for place in GATHER[step]:
                    arrive(place)
        remote(others(k), others(k), ag_send.at[0], ag_other.at[k], "side").wait_recv()
        tab = table[k]
        for n in range(pieces):
            fs = slice(n * cols, (n + 1) * cols)
            raw = lax.dot_general(tab, emb[fs, :], NT, preferred_element_type=F32)
            low = raw[:BLK] * (temper * LOG2E) + bias[k, 0:1, fs]
            high = raw[BLK:] * (temper * LOG2E) + bias[k, 1:2, fs]
            scores[k, :BLK, fs] = low
            scores[k, BLK:, fs] = high
            peak = jnp.maximum(
                jnp.max(low, axis=0, keepdims=True), jnp.max(high, axis=0, keepdims=True)
            )
            before = top[:, fs]
            after = jnp.maximum(before, peak)
            gained = jnp.sum(jnp.exp2(low - after), axis=0, keepdims=True) + jnp.sum(
                jnp.exp2(high - after), axis=0, keepdims=True
            )
            total[:, fs] = total[:, fs] * jnp.exp2(before - after) + gained
            top[:, fs] = after
        table_t[:, pl.ds(pl.multiple_of(k * 2 * BLK, 2 * BLK), 2 * BLK)] = tab.T

    shift[...] = top[...] + jnp.log(total[...]) * LOG2E
    for b in range(blocks):
        fs = slice(b * BLK, (b + 1) * BLK)
        kept = jnp.where(label == tgt[b : b + 1, :], scores[0, 0:BLK, fs], 0.0)
        positive = jnp.sum(kept, axis=0, keepdims=True)
        loss[b : b + 1, :] = (shift[:, fs] - positive) * LN2

    def landed(name):
        i = LAND[name]
        remote(rx.at[i], rx.at[i], ag_send.at[0], rs_recv.at[i], "side").wait_recv()
        return rx[i].astype(F32)

    def gathered(place):
        k = POS[place]
        remote(side_rx.at[k], side_rx.at[k], ag_send.at[0], side_recv.at[k], "side").wait_recv()
        return part[k] + side_rx[k].astype(F32)

    def combine(place):
        takes, name, land = COMBINE[place]
        value = gathered(place)
        for take in takes:
            value = value + landed(take)
        i = LAND[land]
        tx[i] = value.astype(BF16)
        remote(tx.at[i], rx.at[i], rs_send.at[i], rs_recv.at[i], name).start()

    def to_side(k):
        return remote(
            side_tx.at[k], side_rx.at[TURN[k]], side_send.at[k], side_recv.at[TURN[k]], "side"
        )

    @pl.loop(0, CHIPS)
    def _(i):
        k = CHIPS - 1 - i
        base = pl.multiple_of(k * 2 * BLK, 2 * BLK)
        for n in range(pieces):
            fs = slice(n * cols, (n + 1) * cols)
            probs[pl.ds(base, 2 * BLK), fs] = jnp.exp2(scores[k, :, fs] - shift[:, fs]).astype(BF16)
        out = jnp.dot(probs[pl.ds(base, 2 * BLK), :], emb[...], preferred_element_type=F32)
        part[k] = out[:BLK]
        side_tx[k] = out[BLK:].astype(BF16)
        for step in range(CHIPS):
            @pl.when(i == step)
            def _():
                to_side(CHIPS - 1 - step).start()
                for place in REDUCE.get(step, []):
                    combine(place)

    own[...] = jnp.dot(onehot[...], emb[...], preferred_element_type=F32)

    @pl.loop(0, pieces)
    def _(n):
        fs = pl.ds(pl.multiple_of(n * cols, cols), cols)
        toward = jnp.dot(table_t[...], probs[:, fs], preferred_element_type=F32)
        chosen = jnp.dot(table_t[:, 0:BLK], onehot[:, fs], preferred_element_type=F32)
        rows = ((toward - chosen) * temper).astype(BF16).T
        grad[fs, :] = lax.dot_general(rows, w[...], NT, preferred_element_type=F32).astype(BF16)
        pltpu.make_async_copy(grad.at[fs], grad_hbm.at[fs], store_sem.at[n]).start()

    value = gathered((0, 0)) - own[...]
    for take in ["p0", "m0", "Am", "Ap"]:
        value = value + landed(take)
    step_grad[...] = value * temper

    for n in range(pieces):
        fs = pl.ds(n * cols, cols)
        pltpu.make_async_copy(grad.at[fs], grad_hbm.at[fs], store_sem.at[n]).wait()
    for i, k in enumerate(sends):
        remote(mine(k), mine(k), ag_send.at[i], ag_mine.at[k], "side").wait_send()
    for i in range(len(LANDS)):
        remote(tx.at[i], rx.at[i], rs_send.at[i], rs_recv.at[i], "side").wait_send()
    for k in range(CHIPS):
        to_side(k).wait_send()


def shards(frames, w_frame, step_emb, targets, tile_frame, tile_step, tile_count):
    n_frames, depth = frames.shape
    steps, width = step_emb.shape
    blocks = n_frames // BLK
    vmem = pl.BlockSpec(memory_space=pltpu.VMEM)
    anywhere = pl.BlockSpec(memory_space=pl.ANY)
    dma = pltpu.SemaphoreType.DMA
    pieces = n_frames // 256
    loss, grad, step_grad = pl.pallas_call(
        kernel,
        name="contrastive",
        out_shape=(
            jax.ShapeDtypeStruct((blocks, BLK), F32),
            jax.ShapeDtypeStruct((n_frames, depth), BF16),
            jax.ShapeDtypeStruct((steps, width), F32),
        ),
        in_specs=[vmem, vmem, vmem, vmem, pl.BlockSpec(memory_space=pltpu.SMEM), anywhere, anywhere],
        out_specs=(vmem, anywhere, vmem),
        scratch_shapes=[
            pltpu.VMEM((n_frames, depth), BF16),
            pltpu.VMEM((depth, width), BF16),
            pltpu.VMEM((n_frames, width), BF16),
            pltpu.VMEM((CHIPS, 2 * BLK, width), BF16),
            pltpu.VMEM((width, CHIPS * 2 * BLK), BF16),
            pltpu.VMEM((CHIPS, 2 * BLK, n_frames), F32),
            pltpu.VMEM((CHIPS * 2 * BLK, n_frames), BF16),
            pltpu.VMEM((CHIPS, 2, n_frames), F32),
            pltpu.VMEM((1, n_frames), F32),
            pltpu.VMEM((1, n_frames), F32),
            pltpu.VMEM((1, n_frames), F32),
            pltpu.VMEM((BLK, n_frames), BF16),
            pltpu.VMEM((BLK, width), F32),
            pltpu.VMEM((CHIPS, BLK, width), F32),
            pltpu.VMEM((CHIPS, BLK, width), BF16),
            pltpu.VMEM((CHIPS, BLK, width), BF16),
            pltpu.VMEM((len(LANDS), BLK, width), BF16),
            pltpu.VMEM((len(LANDS), BLK, width), BF16),
            pltpu.VMEM((n_frames, depth), BF16),
            dma((2,)),
            dma((31,)),
            dma((CHIPS,)),
            dma((CHIPS,)),
            dma((len(LANDS),)),
            dma((len(LANDS),)),
            dma((CHIPS,)),
            dma((CHIPS,)),
            dma((pieces,)),
        ],
        compiler_params=pltpu.CompilerParams(
            collective_id=0, has_side_effects=True, vmem_limit_bytes=60 * 1024 * 1024
        ),
    )(
        step_emb, targets.reshape(blocks, BLK), tile_frame, tile_step, tile_count, frames, w_frame,
    )
    return (loss.reshape(n_frames), grad, step_grad)


def solution(mesh):
    placed = (
        P(("grp", "vid"), None),
        P(),
        P(("grp", "vid"), None),
        P(("grp", "vid")),
        P(("grp", "vid"), None),
        P(("grp", "vid"), None),
        P(("grp", "vid")),
    )
    return jax.shard_map(
        shards,
        mesh=mesh,
        in_specs=placed,
        out_specs=(P(("grp", "vid")), P(("grp", "vid"), None), P(("grp", "vid"), None)),
        check_vma=False,
    )
```

time: 628 us -> 66.9 us (0.11)
  matrix products: 243 us -> 0 us
  local copies, waits for them, and re-layouts: 131 us -> 5.1 us
  waiting for transfers between devices: 112 us -> 0 us
  loops' own time: 85.7 us -> 0 us
  Pallas kernels: 0 us -> 60.3 us
  other arithmetic: 37.1 us -> 0 us
  between operations: 14.1 us -> 1.29 us
    dot_general x116 -> x0, matrix products: 243 us -> none  [the longest x16 93.2 us: backward_turn(): lax.dot_general(picker.astype(jnp.float32), toward_cols.reshape(blocks, s...]
    while x192 -> x0, local copies, waits for them, and re-layouts: 94.2 us -> none
    another operation x2 -> x0, loops' own time: 85.7 us -> none  [the longest x1 43.3 us: shards(): lax.scan(backward_turn, (start_frames, start_steps), jnp.arange(rounds, d...]
    reduce_scatter x1 -> x0, waiting for transfers between devices: 71.4 us -> none  [shards(): lax.psum_scatter(flat_steps.astype(jnp.bfloat16), 'vid', scatter_dimensio...]
    pallas_call x0 -> x1, Pallas kernels: none -> 60.3 us  [shards(): pl.pallas_call(kernel, name='contrastive', out_shape=(jax.ShapeDtypeStruc...]
    all_gather x1 -> x0, waiting for transfers between devices: 40.1 us -> none  [shards(): table = lax.all_gather(step_emb, 'vid', axis=0, tiled=True)]
    convert_element_type x33 -> x0, other arithmetic: 26.6 us -> none  [the longest x32 20.8 us: round_scores(): slot_ok = (turn * blocks + block_ids < count).astype(jnp.int32)]
    dynamic_slice x32 -> x0, local copies, waits for them, and re-layouts: 18.7 us -> none  [shards(): lax.scan(forward_turn, (start_best, start_total), jnp.arange(rounds, dtyp...]
  transfers between devices with their start and end apart: 2 -> 0, of which waited for: 2 -> 0; matrix products, arithmetic and copies ran while one was open for 3% -> 0% of each run, Pallas kernels for 0% -> 0%
where the time goes in v1:
time: 66.9 us; the launch traced here: 66.7 us
  Pallas kernels  60.3 us (90%)
  local copies, waits for them, and re-layouts  5.1 us (8%)
  between operations  1.29 us (2%)
    pallas_call x1, Pallas kernels, shards(): pl.pallas_call(kernel, name='contrastive', out_shape=(jax.ShapeDtypeStruc...  60.3 us
    unnamed x5, local copies, waits for them, and re-layouts  5.1 us

profile of v1, /device:TPU:1, one launch (start us, length us, event | category | flops | bytes accessed | tf_op | source)
XLA Modules:
  0.0 66.7 jit_solution(11670470242652708683)
XLA Ops:
  1.3 60.3 %contrastive.1 = (f32[8,128]{1,0:T(8,128)}, bf16[1024,1024]{1,0:T(8,128)(2,1)}, f32[128,512]{1,0:T(8,128)}) custom-call(bf16[128,512]{1,0:T(8,128)(2,1)} %step_in.1, s32[8,128]{1,0:T(8,128)} %bitcast.2, s32[1,128]{1,0:T(1,128)} %tile_frame.1, s32[1,128]{1,0:T(1,128)} %tile_step.1, s32[1]{0:T(128)S(6)} %copy.13.count, bf16[1024,1024]{1,0:T(8,128)(2,1)} %frames_hbm.1, ...), custom_call_target="tpu_custom_call" | custom-call | tf_op jit(solution)/shard_map/contrastive/pallas_call | solution.py:300
  61.6 1.3 %copy.14 = f32[1024]{0:T(1024)} copy(f32[1024]{0:T(1024)} %bitcast.3) | data formatting | bytes 8192
  62.9 0.0 copy-start
  62.9 3.1 %copy.15 = bf16[1024,1024]{1,0:T(8,128)(2,1)} copy(bf16[1024,1024]{1,0:T(8,128)(2,1)} %get-tuple-element.13) | data formatting | bytes 4194304
  66.0 0.0 copy-done
  66.0 0.7 %copy.16 = f32[128,512]{1,0:T(8,128)} copy(f32[128,512]{1,0:T(8,128)S(1)} %copy-done) | data formatting | bytes 524288
Async XLA Ops:
  62.9 3.1 %copy-start = (f32[128,512]{1,0:T(8,128)S(1)}, f32[128,512]{1,0:T(8,128)}, u32[]{:S(2)}) copy-start(f32[128,512]{1,0:T(8,128)} %get-tuple-element.14) | copy-start | bytes 786436

commit v2 on v1

--- a/solution.py
+++ b/solution.py
@@ -27,14 +27,17 @@
 TURN = [POS[(db, da)] for da, db in ORDER]
 
 GATHER = {
-    0: [(3, 0), (1, 0), (0, 3), (0, 1)],
-    3: [(2, 0), (3, 3), (1, 1), (3, 1), (1, 3), (0, 2)],
-    10: [(2, 1), (2, 3), (1, 2), (3, 2)],
-    14: [(2, 2)],
+    0: [(3, 0), (1, 0), (2, 0), (0, 3), (0, 1)],
+    3: [(3, 3), (3, 1)],
+    4: [(1, 1), (1, 3)],
+    5: [(2, 1), (2, 3)],
+    7: [(0, 2)],
+    8: [(3, 2), (1, 2)],
+    11: [(2, 2)],
 }
 ONWARD = {
-    (0, 0): ["a+", "a-", "b+", "b-"],
-    (3, 0): ["a+", "b+", "b-"],
+    (0, 0): ["a2", "a+", "a-", "b+", "b-"],
+    (3, 0): ["b+", "b-"],
     (1, 0): ["b+", "b-"],
     (2, 0): ["b+", "b-"],
     (0, 3): ["b+"],
@@ -42,10 +45,10 @@
     (2, 1): ["b-"],
     (3, 1): ["b-"],
 }
-SHIFT = {"a+": (-1, 0), "a-": (1, 0), "b+": (0, -1), "b-": (0, 1)}
+SHIFT = {"a+": (-1, 0), "a-": (1, 0), "a2": (-2, 0), "b+": (0, -1), "b-": (0, 1)}
 
 LANDS = ["h0", "h1", "h2", "h3", "p0", "p1", "p2", "p3",
-         "m0", "m1", "m2", "m3", "A", "Ap", "Am"]
+         "m0", "m1", "m2", "m3", "A2", "Ap", "Am"]
 LAND = {name: i for i, name in enumerate(LANDS)}
 COMBINE = {
     (2, 2): ([], "b-", "h2"),
@@ -60,33 +63,35 @@
     (3, 1): ([], "b+", "p3"),
     (1, 1): (["h1"], "b+", "p1"),
     (0, 1): (["h0"], "b+", "p0"),
-    (2, 0): (["p2", "m2"], "a+", "A"),
-    (1, 0): (["p1", "m1", "A"], "a+", "Ap"),
+    (2, 0): (["p2", "m2"], "a2", "A2"),
+    (1, 0): (["p1", "m1"], "a+", "Ap"),
     (3, 0): (["p3", "m3"], "a-", "Am"),
 }
 REDUCE = {
-    1: [(2, 2)],
-    3: [(3, 2)],
-    4: [(2, 3)],
-    5: [(2, 1), (1, 2)],
-    7: [(0, 2)],
-    8: [(2, 0)],
-    9: [(1, 3), (3, 1)],
-    10: [(3, 3)],
-    11: [(1, 1)],
-    13: [(3, 0), (0, 3)],
-    14: [(0, 1)],
-    15: [(1, 0)],
+    4: [(2, 2)],
+    6: [(3, 2)],
+    8: [(2, 1), (1, 2)],
+    10: [(0, 2)],
+    12: [(3, 1), (1, 3), (2, 3)],
+    13: [(3, 3)],
+    14: [(1, 1)],
 }
+REDUCE_LATE = {
+    (0, 0): [(0, 3)],
+    (0, 1): [(0, 1)],
+    (1, 0): [(2, 0)],
+    (1, 1): [(3, 0), (1, 0)],
+}
+EARLY = 8
+LATE = CHIPS - EARLY
 
 
 def kernel(
     step_in, tgt, tile_frame, tile_step, count, frames_hbm, w_hbm,
-    loss, grad_hbm, step_grad,
-    frames, w, emb, table, table_t, scores, probs, bias, top, total, shift,
-    onehot, own, part, side_tx, side_rx, tx, rx, grad,
+    loss, grad, step_grad,
+    frames, w, emb, table, table_t, step_t, scores, probs, near, toward, bias, top, total,
+    shift, onehot, own, turned_rows, part, side_tx, side_rx, tx, rx,
     load_sem, ag_send, ag_mine, ag_other, rs_send, rs_recv, side_send, side_recv,
-    store_sem,
 ):
     n_frames, width = emb.shape
     blocks = n_frames // BLK
@@ -106,7 +111,7 @@
         return (ya * SIDE + zb) * 2 + kind
 
     dev = {
-        "a+": owner(1, 0, 0), "a-": owner(3, 0, 0),
+        "a+": owner(1, 0, 0), "a-": owner(3, 0, 0), "a2": owner(2, 0, 0),
         "b+": owner(0, 1, 0), "b-": owner(0, 3, 0),
         "side": owner(0, 0, 1),
     }
@@ -120,41 +125,6 @@
     for name in dev:
         pl.semaphore_signal(barrier, inc=1, device_id={"vid": dev[name]}, device_id_type=MESH)
     table[0, 0:BLK, :] = step_in[...]
-    pl.semaphore_wait(barrier, len(dev))
-
-    def mine(k):
-        return table.at[k, pl.ds(0, BLK)]
-
-    def others(k):
-        return table.at[k, pl.ds(BLK, BLK)]
-
-    def remote(src, dst, send, recv, name):
-        return pltpu.make_async_remote_copy(
-            src_ref=src, dst_ref=dst, send_sem=send, recv_sem=recv,
-            device_id={"vid": dev[name]}, device_id_type=MESH,
-        )
-
-    sends = []
-
-    def pass_on(place):
-        k = POS[place]
-        for name in ONWARD.get(place, []):
-            sa, sb = SHIFT[name]
-            land = POS[((place[0] + sa) % SIDE, (place[1] + sb) % SIDE)]
-            sends.append(k)
-            remote(mine(k), mine(land), ag_send.at[len(sends) - 1], ag_mine.at[land], name).start()
-        sends.append(k)
-        remote(
-            mine(k), others(TURN[k]), ag_send.at[len(sends) - 1], ag_other.at[TURN[k]], "side"
-        ).start()
-
-    def arrive(place):
-        k = POS[place]
-        remote(mine(k), mine(k), ag_send.at[0], ag_mine.at[k], "side").wait_recv()
-        pass_on(place)
-
-    pass_on((0, 0))
-
     row = lax.broadcasted_iota(jnp.int32, (2 * CHIPS, BLK), 0)
     ids = jnp.zeros((2 * CHIPS, BLK), jnp.int32)
     for k, (da, db) in enumerate(ORDER):
@@ -164,7 +134,7 @@
     block_of = lax.broadcasted_iota(jnp.int32, (n_frames, BLK), 0) // BLK
     slot = lax.broadcasted_iota(jnp.int32, (n_frames, BLK), 1)
     frame_hot = jnp.where(
-        (block_of == tile_frame[...]) & (slot < count[0]), 1.0, 0.0
+        (block_of == tile_frame[...]) & (slot < count[...]), 1.0, 0.0
     ).astype(BF16)
     seen = lax.dot_general(step_hot, frame_hot, NT, preferred_element_type=F32)
     hidden = jnp.where(seen > 0.5, 0.0, FAR)
@@ -178,6 +148,43 @@
     top[...] = jnp.full_like(top, FAR)
     total[...] = jnp.zeros_like(total)
 
+    toward[...] = jnp.zeros_like(toward)
+    step_t[...] = step_in[...].T
+    pl.semaphore_wait(barrier, len(dev))
+
+    def mine(k):
+        return table.at[k, pl.ds(0, BLK)]
+
+    def others(k):
+        return table.at[k, pl.ds(BLK, BLK)]
+
+    def remote(src, dst, send, recv, name):
+        return pltpu.make_async_remote_copy(
+            src_ref=src, dst_ref=dst, send_sem=send, recv_sem=recv,
+            device_id={"vid": dev[name]}, device_id_type=MESH,
+        )
+
+    sends = []
+
+    def pass_on(place):
+        k = POS[place]
+        for name in ONWARD.get(place, []):
+            sa, sb = SHIFT[name]
+            land = POS[((place[0] + sa) % SIDE, (place[1] + sb) % SIDE)]
+            sends.append(k)
+            remote(mine(k), mine(land), ag_send.at[len(sends) - 1], ag_mine.at[land], name).start()
+        sends.append(k)
+        remote(
+            mine(k), others(TURN[k]), ag_send.at[len(sends) - 1], ag_other.at[TURN[k]], "side"
+        ).start()
+
+    def arrive(place):
+        k = POS[place]
+        remote(mine(k), mine(k), ag_send.at[0], ag_mine.at[k], "side").wait_recv()
+        pass_on(place)
+
+    pass_on((0, 0))
+
     load_frames.wait()
     load_w.wait()
     for n in range(pieces):
@@ -186,15 +193,19 @@
             frames[rows, :], w[...], preferred_element_type=F32
         ).astype(BF16)
 
-    @pl.loop(0, CHIPS)
-    def _(k):
+    def score(k, early):
         for step in GATHER:
-            @pl.when(k == step)
-            def _():
-                for place in GATHER[step]:
-                    arrive(place)
+            if (step < EARLY) == early:
+                @pl.when(k == step)
+                def _():
+                    for place in GATHER[step]:
+                        arrive(place)
         remote(others(k), others(k), ag_send.at[0], ag_other.at[k], "side").wait_recv()
         tab = table[k]
+        turned = tab.T
+        if not early:
+            base = pl.multiple_of((k - EARLY) * 2 * BLK, 2 * BLK)
+            table_t[:, pl.ds(base, 2 * BLK)] = turned
         for n in range(pieces):
             fs = slice(n * cols, (n + 1) * cols)
             raw = lax.dot_general(tab, emb[fs, :], NT, preferred_element_type=F32)
@@ -207,14 +218,32 @@
             )
             before = top[:, fs]
             after = jnp.maximum(before, peak)
-            gained = jnp.sum(jnp.exp2(low - after), axis=0, keepdims=True) + jnp.sum(
-                jnp.exp2(high - after), axis=0, keepdims=True
-            )
-            total[:, fs] = total[:, fs] * jnp.exp2(before - after) + gained
+            fade = jnp.exp2(before - after)
+            low = jnp.exp2(low - after)
+            high = jnp.exp2(high - after)
+            gained = jnp.sum(low, axis=0, keepdims=True) + jnp.sum(high, axis=0, keepdims=True)
+            total[:, fs] = total[:, fs] * fade + gained
             top[:, fs] = after
-        table_t[:, pl.ds(pl.multiple_of(k * 2 * BLK, 2 * BLK), 2 * BLK)] = tab.T
-
-    shift[...] = top[...] + jnp.log(total[...]) * LOG2E
+            if early:
+                near[:BLK, fs] = low.astype(BF16)
+                near[BLK:, fs] = high.astype(BF16)
+                toward[:, fs] = toward[:, fs] * fade + jnp.dot(
+                    turned, near[:, fs], preferred_element_type=F32
+                )
+
+    @pl.loop(0, EARLY)
+    def _(k):
+        score(k, True)
+
+    shift[...] = top[...]
+
+    @pl.loop(EARLY, CHIPS)
+    def _(k):
+        score(k, False)
+
+    lse = top[...] + jnp.log(total[...]) * LOG2E
+    top[...] = jnp.exp2(shift[...] - lse)
+    shift[...] = lse
     for b in range(blocks):
         fs = slice(b * BLK, (b + 1) * BLK)
         kept = jnp.where(label == tgt[b : b + 1, :], scores[0, 0:BLK, fs], 0.0)
@@ -266,27 +295,54 @@
 
     @pl.loop(0, pieces)
     def _(n):
+        for (piece, half), places in REDUCE_LATE.items():
+            if half == 0:
+                @pl.when(n == piece)
+                def _():
+                    for place in places:
+                        combine(place)
         fs = pl.ds(pl.multiple_of(n * cols, cols), cols)
-        toward = jnp.dot(table_t[...], probs[:, fs], preferred_element_type=F32)
-        chosen = jnp.dot(table_t[:, 0:BLK], onehot[:, fs], preferred_element_type=F32)
-        rows = ((toward - chosen) * temper).astype(BF16).T
-        grad[fs, :] = lax.dot_general(rows, w[...], NT, preferred_element_type=F32).astype(BF16)
-        pltpu.make_async_copy(grad.at[fs], grad_hbm.at[fs], store_sem.at[n]).start()
+        rows = toward[:, fs] * top[:, fs] - jnp.dot(
+            step_t[...], onehot[:, fs], preferred_element_type=F32
+        )
+        rows = rows + jnp.dot(
+            table_t[...], probs[EARLY * 2 * BLK :, fs], preferred_element_type=F32
+        )
+        rows_t = (rows * temper).astype(BF16).T
+        turned_rows[...] = rows_t
+        for (piece, half), places in REDUCE_LATE.items():
+            if half == 1:
+                @pl.when(n == piece)
+                def _():
+                    for place in places:
+                        combine(place)
+        grad[fs, :] = lax.dot_general(
+            turned_rows[...], w[...], NT, preferred_element_type=F32
+        ).astype(BF16)
 
     value = gathered((0, 0)) - own[...]
-    for take in ["p0", "m0", "Am", "Ap"]:
+    for take in ["p0", "m0", "Am", "A2", "Ap"]:
         value = value + landed(take)
     step_grad[...] = value * temper
 
-    for n in range(pieces):
-        fs = pl.ds(n * cols, cols)
-        pltpu.make_async_copy(grad.at[fs], grad_hbm.at[fs], store_sem.at[n]).wait()
     for i, k in enumerate(sends):
         remote(mine(k), mine(k), ag_send.at[i], ag_mine.at[k], "side").wait_send()
     for i in range(len(LANDS)):
         remote(tx.at[i], rx.at[i], rs_send.at[i], rs_recv.at[i], "side").wait_send()
     for k in range(CHIPS):
         to_side(k).wait_send()
+
+
+def hand_over(loss, grad, step_grad, loss_out, grad_out, step_grad_out, sem):
+    copies = [
+        pltpu.make_async_copy(grad, grad_out, sem.at[0]),
+        pltpu.make_async_copy(step_grad, step_grad_out, sem.at[1]),
+        pltpu.make_async_copy(loss, loss_out, sem.at[2]),
+    ]
+    for copy in copies:
+        copy.start()
+    for copy in copies:
+        copy.wait()
 
 
 def shards(frames, w_frame, step_emb, targets, tile_frame, tile_step, tile_count):
@@ -296,37 +352,41 @@
     vmem = pl.BlockSpec(memory_space=pltpu.VMEM)
     anywhere = pl.BlockSpec(memory_space=pl.ANY)
     dma = pltpu.SemaphoreType.DMA
-    pieces = n_frames // 256
-    loss, grad, step_grad = pl.pallas_call(
+    results = (
+        jax.ShapeDtypeStruct((blocks, BLK), F32),
+        jax.ShapeDtypeStruct((n_frames, depth), BF16),
+        jax.ShapeDtypeStruct((steps, width), F32),
+    )
+    held = tuple(pltpu.VMEM(r.shape, r.dtype) for r in results)
+    found = pl.pallas_call(
         kernel,
         name="contrastive",
-        out_shape=(
-            jax.ShapeDtypeStruct((blocks, BLK), F32),
-            jax.ShapeDtypeStruct((n_frames, depth), BF16),
-            jax.ShapeDtypeStruct((steps, width), F32),
-        ),
-        in_specs=[vmem, vmem, vmem, vmem, pl.BlockSpec(memory_space=pltpu.SMEM), anywhere, anywhere],
-        out_specs=(vmem, anywhere, vmem),
+        out_shape=held,
+        in_specs=[vmem] * 5 + [anywhere] * 2,
+        out_specs=(vmem,) * 3,
         scratch_shapes=[
             pltpu.VMEM((n_frames, depth), BF16),
             pltpu.VMEM((depth, width), BF16),
             pltpu.VMEM((n_frames, width), BF16),
             pltpu.VMEM((CHIPS, 2 * BLK, width), BF16),
-            pltpu.VMEM((width, CHIPS * 2 * BLK), BF16),
+            pltpu.VMEM((width, LATE * 2 * BLK), BF16),
+            pltpu.VMEM((width, BLK), BF16),
             pltpu.VMEM((CHIPS, 2 * BLK, n_frames), F32),
             pltpu.VMEM((CHIPS * 2 * BLK, n_frames), BF16),
+            pltpu.VMEM((2 * BLK, n_frames), BF16),
+            pltpu.VMEM((width, n_frames), F32),
             pltpu.VMEM((CHIPS, 2, n_frames), F32),
             pltpu.VMEM((1, n_frames), F32),
             pltpu.VMEM((1, n_frames), F32),
             pltpu.VMEM((1, n_frames), F32),
             pltpu.VMEM((BLK, n_frames), BF16),
             pltpu.VMEM((BLK, width), F32),
+            pltpu.VMEM((2 * BLK, width), BF16),
             pltpu.VMEM((CHIPS, BLK, width), F32),
             pltpu.VMEM((CHIPS, BLK, width), BF16),
             pltpu.VMEM((CHIPS, BLK, width), BF16),
             pltpu.VMEM((len(LANDS), BLK, width), BF16),
             pltpu.VMEM((len(LANDS), BLK, width), BF16),
-            pltpu.VMEM((n_frames, depth), BF16),
             dma((2,)),
             dma((31,)),
             dma((CHIPS,)),
@@ -335,14 +395,22 @@
             dma((len(LANDS),)),
             dma((CHIPS,)),
             dma((CHIPS,)),
-            dma((pieces,)),
         ],
         compiler_params=pltpu.CompilerParams(
-            collective_id=0, has_side_effects=True, vmem_limit_bytes=60 * 1024 * 1024
+            collective_id=0, has_side_effects=True, vmem_limit_bytes=54 * 1024 * 1024
         ),
     )(
-        step_emb, targets.reshape(blocks, BLK), tile_frame, tile_step, tile_count, frames, w_frame,
+        step_emb, targets.reshape(blocks, BLK), tile_frame, tile_step,
+        tile_count.reshape(1, 1), frames, w_frame,
     )
+    loss, grad, step_grad = pl.pallas_call(
+        hand_over,
+        name="hand_over",
+        out_shape=results,
+        in_specs=[pl.BlockSpec(memory_space=pltpu.VMEM)] * 3,
+        out_specs=(anywhere,) * 3,
+        scratch_shapes=[dma((3,))],
+    )(*[pltpu.with_memory_space_constraint(f, pltpu.VMEM) for f in found])
     return (loss.reshape(n_frames), grad, step_grad)
 
 

time: 66.9 us -> 53.9 us (0.81)
  Pallas kernels: 60.3 us -> 52.4 us
  local copies, waits for them, and re-layouts: 5.1 us -> 0 us
    pallas_call x1 -> x2, Pallas kernels: 60.3 us -> 52.4 us  [the longest x1 50.9 us: shards(): pl.pallas_call(kernel, name='contrastive', out_shape=held, in_specs=[vmem...]
    unnamed x5 -> x0, local copies, waits for them, and re-layouts: 5.1 us -> none
where the time goes in v2:
time: 53.9 us; the launch traced here: 53.6 us
  Pallas kernels  52.4 us (97%)
  between operations  1.29 us (2%)
    pallas_call x1, Pallas kernels, shards(): pl.pallas_call(kernel, name='contrastive', out_shape=held, in_specs=[vmem...  50.9 us
    pallas_call x1, Pallas kernels, shards(): pl.pallas_call(hand_over, name='hand_over', out_shape=results, in_specs=[...  1.42 us

profile of v2, /device:TPU:1, one launch (start us, length us, event | category | flops | bytes accessed | tf_op | source)
XLA Modules:
  0.0 53.6 jit_solution(17988416624493191095)
XLA Ops:
  1.3 50.9 %contrastive.1 = (f32[8,128]{1,0:T(8,128)S(1)}, bf16[1024,1024]{1,0:T(8,128)(2,1)S(1)}, f32[128,512]{1,0:T(8,128)S(1)}) custom-call(bf16[128,512]{1,0:T(8,128)(2,1)} %step_in.1, s32[8,128]{1,0:T(8,128)} %bitcast.4, s32[1,128]{1,0:T(1,128)} %tile_frame.1, s32[1,128]{1,0:T(1,128)} %tile_step.1, s32[1,1]{1,0:T(1,128)} %bitcast.3.count, ...), custom_call_target="tpu_custom_call" | custom-call | tf_op jit(solution)/shard_map/contrastive/pallas_call | solution.py:361
  52.2 1.4 %hand_over.1 = (f32[8,128]{1,0:T(8,128)}, bf16[1024,1024]{1,0:T(8,128)(2,1)}, f32[128,512]{1,0:T(8,128)}) custom-call(f32[8,128]{1,0:T(8,128)S(1)} %get-tuple-element.9.loss, bf16[1024,1024]{1,0:T(8,128)(2,1)S(1)} %get-tuple-element.10.grad, f32[128,512]{1,0:T(8,128)S(1)} %get-tuple-element.11.step_grad), custom_call_target="tpu_custom_call" | custom-call | tf_op jit(solution)/shard_map/hand_over/pallas_call | solution.py:406

commit v3 on v2

--- a/solution.py
+++ b/solution.py
@@ -26,15 +26,7 @@
 POS = {place: k for k, place in enumerate(ORDER)}
 TURN = [POS[(db, da)] for da, db in ORDER]
 
-GATHER = {
-    0: [(3, 0), (1, 0), (2, 0), (0, 3), (0, 1)],
-    3: [(3, 3), (3, 1)],
-    4: [(1, 1), (1, 3)],
-    5: [(2, 1), (2, 3)],
-    7: [(0, 2)],
-    8: [(3, 2), (1, 2)],
-    11: [(2, 2)],
-}
+GATHER = {1: [(3, 0), (1, 0), (2, 0), (0, 3), (0, 1)], 3: [(3, 3), (3, 1)], 4: [(1, 1), (1, 3)], 5: [(2, 1), (2, 3)], 7: [(0, 2)], 8: [(3, 2), (1, 2)], 11: [(2, 2)]}
 ONWARD = {
     (0, 0): ["a2", "a+", "a-", "b+", "b-"],
     (3, 0): ["b+", "b-"],
@@ -45,7 +37,7 @@
     (2, 1): ["b-"],
     (3, 1): ["b-"],
 }
-SHIFT = {"a+": (-1, 0), "a-": (1, 0), "a2": (-2, 0), "b+": (0, -1), "b-": (0, 1)}
+SHIFT = {"a+": (-1, 0), "a-": (1, 0), "a2": (-2, 0), "b+": (0, -1), "b-": (0, 1), "b2": (0, -2)}
 
 LANDS = ["h0", "h1", "h2", "h3", "p0", "p1", "p2", "p3",
          "m0", "m1", "m2", "m3", "A2", "Ap", "Am"]
@@ -82,15 +74,17 @@
     (1, 0): [(2, 0)],
     (1, 1): [(3, 0), (1, 0)],
 }
-EARLY = 8
+EARLY = 4
 LATE = CHIPS - EARLY
+GROUP = 1
 
 
 def kernel(
-    step_in, tgt, tile_frame, tile_step, count, frames_hbm, w_hbm,
+    step_hbm, tgt_hbm, tile_frame_hbm, tile_step_hbm, count_hbm, frames_hbm, w_hbm,
     loss, grad, step_grad,
     frames, w, emb, table, table_t, step_t, scores, probs, near, toward, bias, top, total,
-    shift, onehot, own, turned_rows, part, side_tx, side_rx, tx, rx,
+    shift, onehot, own, turned_rows, part, side_tx, side_rx, tx, rx, emb_t,
+    tgt, tile_frame, tile_step, count,
     load_sem, ag_send, ag_mine, ag_other, rs_send, rs_recv, side_send, side_recv,
 ):
     n_frames, width = emb.shape
@@ -112,19 +106,27 @@
 
     dev = {
         "a+": owner(1, 0, 0), "a-": owner(3, 0, 0), "a2": owner(2, 0, 0),
-        "b+": owner(0, 1, 0), "b-": owner(0, 3, 0),
+        "b+": owner(0, 1, 0), "b-": owner(0, 3, 0), "b2": owner(0, 2, 0),
         "side": owner(0, 0, 1),
     }
-
-    load_frames = pltpu.make_async_copy(frames_hbm, frames, load_sem.at[0])
-    load_w = pltpu.make_async_copy(w_hbm, w, load_sem.at[1])
-    load_frames.start()
-    load_w.start()
 
     barrier = pltpu.get_barrier_semaphore()
     for name in dev:
         pl.semaphore_signal(barrier, inc=1, device_id={"vid": dev[name]}, device_id_type=MESH)
-    table[0, 0:BLK, :] = step_in[...]
+    loads = [
+        pltpu.make_async_copy(src, dst, load_sem.at[i])
+        for i, (src, dst) in enumerate([
+            (tile_frame_hbm, tile_frame), (tile_step_hbm, tile_step), (count_hbm, count),
+            (tgt_hbm, tgt), (step_hbm, table.at[0, pl.ds(0, BLK)]),
+            (frames_hbm, frames), (w_hbm, w),
+        ])
+    ]
+    for load in loads:
+        load.start()
+    toward[...] = jnp.zeros_like(toward)
+    for load in loads[:5]:
+        load.wait()
+
     row = lax.broadcasted_iota(jnp.int32, (2 * CHIPS, BLK), 0)
     ids = jnp.zeros((2 * CHIPS, BLK), jnp.int32)
     for k, (da, db) in enumerate(ORDER):
@@ -148,8 +150,7 @@
     top[...] = jnp.full_like(top, FAR)
     total[...] = jnp.zeros_like(total)
 
-    toward[...] = jnp.zeros_like(toward)
-    step_t[...] = step_in[...].T
+    step_t[...] = table[0, 0:BLK, :].T
     pl.semaphore_wait(barrier, len(dev))
 
     def mine(k):
@@ -185,59 +186,69 @@
 
     pass_on((0, 0))
 
-    load_frames.wait()
-    load_w.wait()
+    for load in loads[5:]:
+        load.wait()
     for n in range(pieces):
         rows = slice(n * cols, (n + 1) * cols)
         emb[rows, :] = jnp.dot(
             frames[rows, :], w[...], preferred_element_type=F32
         ).astype(BF16)
+        emb_t[:, rows] = emb[rows, :].T
 
     def score(k, early):
         for step in GATHER:
-            if (step < EARLY) == early:
+            if (step * GROUP < EARLY) == early:
                 @pl.when(k == step)
                 def _():
                     for place in GATHER[step]:
                         arrive(place)
-        remote(others(k), others(k), ag_send.at[0], ag_other.at[k], "side").wait_recv()
-        tab = table[k]
-        turned = tab.T
+        tabs, turns = [], []
+        for g in range(GROUP):
+            j = k * GROUP + g
+            remote(others(j), others(j), ag_send.at[0], ag_other.at[j], "side").wait_recv()
+            tabs.append(table[j])
+            turns.append(tabs[-1].T)
+        tab = jnp.concatenate(tabs, axis=0)
+        turned = jnp.concatenate(turns, axis=1)
+        tall = 2 * BLK * GROUP
         if not early:
-            base = pl.multiple_of((k - EARLY) * 2 * BLK, 2 * BLK)
-            table_t[:, pl.ds(base, 2 * BLK)] = turned
+            base = pl.multiple_of((k * GROUP - EARLY) * 2 * BLK, tall)
+            table_t[:, pl.ds(base, tall)] = turned
         for n in range(pieces):
             fs = slice(n * cols, (n + 1) * cols)
-            raw = lax.dot_general(tab, emb[fs, :], NT, preferred_element_type=F32)
-            low = raw[:BLK] * (temper * LOG2E) + bias[k, 0:1, fs]
-            high = raw[BLK:] * (temper * LOG2E) + bias[k, 1:2, fs]
-            scores[k, :BLK, fs] = low
-            scores[k, BLK:, fs] = high
-            peak = jnp.maximum(
-                jnp.max(low, axis=0, keepdims=True), jnp.max(high, axis=0, keepdims=True)
-            )
+            raw = jnp.dot(tab, emb_t[:, fs], preferred_element_type=F32)
+            parts = []
             before = top[:, fs]
-            after = jnp.maximum(before, peak)
+            after = before
+            for g in range(2 * GROUP):
+                j, h = g // 2, g % 2
+                value = raw[g * BLK : (g + 1) * BLK] * (temper * LOG2E) + bias[
+                    k * GROUP + j, h : h + 1, fs
+                ]
+                scores[k * GROUP + j, h * BLK : (h + 1) * BLK, fs] = value
+                after = jnp.maximum(after, jnp.max(value, axis=0, keepdims=True))
+                parts.append(value)
             fade = jnp.exp2(before - after)
-            low = jnp.exp2(low - after)
-            high = jnp.exp2(high - after)
-            gained = jnp.sum(low, axis=0, keepdims=True) + jnp.sum(high, axis=0, keepdims=True)
-            total[:, fs] = total[:, fs] * fade + gained
+            gained = total[:, fs] * fade
+            for g in range(2 * GROUP):
+                value = jnp.exp2(parts[g] - after)
+                gained = gained + jnp.sum(value, axis=0, keepdims=True)
+                if early:
+                    near[g * BLK : (g + 1) * BLK, fs] = value.astype(BF16)
+            total[:, fs] = gained
             top[:, fs] = after
             if early:
-                near[:BLK, fs] = low.astype(BF16)
-                near[BLK:, fs] = high.astype(BF16)
                 toward[:, fs] = toward[:, fs] * fade + jnp.dot(
                     turned, near[:, fs], preferred_element_type=F32
                 )
 
-    @pl.loop(0, EARLY)
+    @pl.loop(0, EARLY // GROUP)
     def _(k):
         score(k, True)
 
     shift[...] = top[...]
 
-    @pl.loop(EARLY, CHIPS)
+    @pl.loop(EARLY // GROUP, CHIPS // GROUP)
     def _(k):
         score(k, False)
 
@@ -362,7 +373,7 @@
         kernel,
         name="contrastive",
         out_shape=held,
-        in_specs=[vmem] * 5 + [anywhere] * 2,
+        in_specs=[anywhere] * 7,
         out_specs=(vmem,) * 3,
         scratch_shapes=[
             pltpu.VMEM((n_frames, depth), BF16),
@@ -373,7 +384,7 @@
             pltpu.VMEM((width, BLK), BF16),
             pltpu.VMEM((CHIPS, 2 * BLK, n_frames), F32),
             pltpu.VMEM((CHIPS * 2 * BLK, n_frames), BF16),
-            pltpu.VMEM((2 * BLK, n_frames), BF16),
+            pltpu.VMEM((GROUP * 2 * BLK, n_frames), BF16),
             pltpu.VMEM((width, n_frames), F32),
             pltpu.VMEM((CHIPS, 2, n_frames), F32),
             pltpu.VMEM((1, n_frames), F32),
@@ -387,7 +398,12 @@
             pltpu.VMEM((CHIPS, BLK, width), BF16),
             pltpu.VMEM((len(LANDS), BLK, width), BF16),
             pltpu.VMEM((len(LANDS), BLK, width), BF16),
-            dma((2,)),
+            pltpu.VMEM((width, n_frames), BF16),
+            pltpu.VMEM((blocks, BLK), jnp.int32),
+            pltpu.VMEM((1, BLK), jnp.int32),
+            pltpu.VMEM((1, BLK), jnp.int32),
+            pltpu.VMEM((1, 1), jnp.int32),
+            dma((7,)),
             dma((31,)),
             dma((CHIPS,)),
             dma((CHIPS,)),

time: 53.9 us -> 51.4 us (0.954)
  Pallas kernels: 52.4 us -> 50 us
    pallas_call x1, Pallas kernels: 50.9 us -> 48.5 us  [shards(): pl.pallas_call(kernel, name='contrastive', out_shape=held, in_specs=[anyw...]
where the time goes in v3:
time: 51.4 us; the launch traced here: 51.2 us
  Pallas kernels  50 us (97%)
  between operations  1.29 us (3%)
    pallas_call x1, Pallas kernels, shards(): pl.pallas_call(kernel, name='contrastive', out_shape=held, in_specs=[anyw...  48.5 us
    pallas_call x1, Pallas kernels, shards(): pl.pallas_call(hand_over, name='hand_over', out_shape=results, in_specs=[...  1.42 us

profile of v3, /device:TPU:1, one launch (start us, length us, event | category | flops | bytes accessed | tf_op | source)
XLA Modules:
  0.0 51.2 jit_solution(949653717174059195)
XLA Ops:
  1.3 48.5 %contrastive.1 = (f32[8,128]{1,0:T(8,128)S(1)}, bf16[1024,1024]{1,0:T(8,128)(2,1)S(1)}, f32[128,512]{1,0:T(8,128)S(1)}) custom-call(bf16[128,512]{1,0:T(8,128)(2,1)} %step_hbm.1, s32[8,128]{1,0:T(8,128)} %bitcast.4, s32[1,128]{1,0:T(1,128)} %tile_frame_hbm.1, s32[1,128]{1,0:T(1,128)} %tile_step_hbm.1, s32[1,1]{1,0:T(1,128)} %bitcast.3.count_hbm, ...), custom_call_target="tpu_custom_call" | custom-call | tf_op jit(solution)/shard_map/contrastive/pallas_call | solution.py:372
  49.8 1.4 %hand_over.1 = (f32[8,128]{1,0:T(8,128)}, bf16[1024,1024]{1,0:T(8,128)(2,1)}, f32[128,512]{1,0:T(8,128)}) custom-call(f32[8,128]{1,0:T(8,128)S(1)} %get-tuple-element.9.loss, bf16[1024,1024]{1,0:T(8,128)(2,1)S(1)} %get-tuple-element.10.grad, f32[128,512]{1,0:T(8,128)S(1)} %get-tuple-element.11.step_grad), custom_call_target="tpu_custom_call" | custom-call | tf_op jit(solution)/shard_map/hand_over/pallas_call | solution.py:422

commit v4 on v3

--- a/solution.py
+++ b/solution.py
@@ -26,9 +26,9 @@
 POS = {place: k for k, place in enumerate(ORDER)}
 TURN = [POS[(db, da)] for da, db in ORDER]
 
-GATHER = {1: [(3, 0), (1, 0), (2, 0), (0, 3), (0, 1)], 3: [(3, 3), (3, 1)], 4: [(1, 1), (1, 3)], 5: [(2, 1), (2, 3)], 7: [(0, 2)], 8: [(3, 2), (1, 2)], 11: [(2, 2)]}
+GATHER = {1: [(3, 0), (1, 0), (0, 3), (0, 1)], 2: [(2, 0)], 3: [(3, 3), (3, 1)], 4: [(1, 1), (1, 3)], 5: [(2, 1), (2, 3)], 7: [(0, 2)], 8: [(3, 2), (1, 2)], 11: [(2, 2)]}
 ONWARD = {
-    (0, 0): ["a2", "a+", "a-", "b+", "b-"],
+    (0, 0): ['a+', 'a-', 'b+', 'b-', 'a2'],
     (3, 0): ["b+", "b-"],
     (1, 0): ["b+", "b-"],
     (2, 0): ["b+", "b-"],
@@ -68,12 +68,7 @@
     13: [(3, 3)],
     14: [(1, 1)],
 }
-REDUCE_LATE = {
-    (0, 0): [(0, 3)],
-    (0, 1): [(0, 1)],
-    (1, 0): [(2, 0)],
-    (1, 1): [(3, 0), (1, 0)],
-}
+REDUCE_LATE = {(0, 0): [(0, 3)], (0, 1): [(0, 1), (2, 0)], (1, 0): [(3, 0), (1, 0)]}
 EARLY = 4
 LATE = CHIPS - EARLY
 GROUP = 1
@@ -285,26 +280,32 @@
             side_tx.at[k], side_rx.at[TURN[k]], side_send.at[k], side_recv.at[TURN[k]], "side"
         )
 
-    @pl.loop(0, CHIPS)
+    @pl.loop(0, CHIPS // 2)
     def _(i):
-        k = CHIPS - 1 - i
-        base = pl.multiple_of(k * 2 * BLK, 2 * BLK)
+        k = CHIPS - 2 - 2 * i
+        tall = 4 * BLK
+        base = pl.multiple_of(k * 2 * BLK, tall)
         for n in range(pieces):
             fs = slice(n * cols, (n + 1) * cols)
-            probs[pl.ds(base, 2 * BLK), fs] = jnp.exp2(scores[k, :, fs] - shift[:, fs]).astype(BF16)
-        out = jnp.dot(probs[pl.ds(base, 2 * BLK), :], emb[...], preferred_element_type=F32)
-        part[k] = out[:BLK]
-        side_tx[k] = out[BLK:].astype(BF16)
-        for step in range(CHIPS):
+            for g in range(2):
+                probs[pl.ds(base + g * 2 * BLK, 2 * BLK), fs] = jnp.exp2(
+                    scores[k + g, :, fs] - shift[:, fs]
+                ).astype(BF16)
+        out = jnp.dot(probs[pl.ds(base, tall), :], emb[...], preferred_element_type=F32)
+        for g in range(2):
+            part[k + g] = out[2 * g * BLK : (2 * g + 1) * BLK]
+            side_tx[k + g] = out[(2 * g + 1) * BLK : (2 * g + 2) * BLK].astype(BF16)
+        for step in range(CHIPS // 2):
             @pl.when(i == step)
             def _():
-                to_side(CHIPS - 1 - step).start()
-                for place in REDUCE.get(step, []):
+                to_side(CHIPS - 1 - 2 * step).start()
+                to_side(CHIPS - 2 - 2 * step).start()
+                for place in REDUCE.get(2 * step, []) + REDUCE.get(2 * step + 1, []):
                     combine(place)
 
     own[...] = jnp.dot(onehot[...], emb[...], preferred_element_type=F32)
 
-    @pl.loop(0, pieces)
+    @pl.loop(0, pieces // 2)
     def _(n):
         for (piece, half), places in REDUCE_LATE.items():
             if half == 0:
@@ -312,7 +313,7 @@
                 def _():
                     for place in places:
                         combine(place)
-        fs = pl.ds(pl.multiple_of(n * cols, cols), cols)
+        fs = pl.ds(pl.multiple_of(n * 2 * cols, 2 * cols), 2 * cols)
         rows = toward[:, fs] * top[:, fs] - jnp.dot(
             step_t[...], onehot[:, fs], preferred_element_type=F32
         )
@@ -392,7 +393,7 @@
             pltpu.VMEM((1, n_frames), F32),
             pltpu.VMEM((BLK, n_frames), BF16),
             pltpu.VMEM((BLK, width), F32),
-            pltpu.VMEM((2 * BLK, width), BF16),
+            pltpu.VMEM((4 * BLK, width), BF16),
             pltpu.VMEM((CHIPS, BLK, width), F32),
             pltpu.VMEM((CHIPS, BLK, width), BF16),
             pltpu.VMEM((CHIPS, BLK, width), BF16),

time: 51.4 us -> 50.3 us (0.979)
  Pallas kernels: 50 us -> 48.9 us
    pallas_call x1, Pallas kernels: 48.5 us -> 47.5 us  [shards(): pl.pallas_call(kernel, name='contrastive', out_shape=held, in_specs=[anyw...]
where the time goes in v4:
time: 50.3 us; the launch traced here: 50.2 us
  Pallas kernels  48.9 us (97%)
  between operations  1.29 us (3%)
    pallas_call x1, Pallas kernels, shards(): pl.pallas_call(kernel, name='contrastive', out_shape=held, in_specs=[anyw...  47.5 us
    pallas_call x1, Pallas kernels, shards(): pl.pallas_call(hand_over, name='hand_over', out_shape=results, in_specs=[...  1.42 us

profile of v4, /device:TPU:1, one launch (start us, length us, event | category | flops | bytes accessed | tf_op | source)
XLA Modules:
  0.0 50.2 jit_solution(7252971357119759114)
XLA Ops:
  1.3 47.5 %contrastive.1 = (f32[8,128]{1,0:T(8,128)S(1)}, bf16[1024,1024]{1,0:T(8,128)(2,1)S(1)}, f32[128,512]{1,0:T(8,128)S(1)}) custom-call(bf16[128,512]{1,0:T(8,128)(2,1)} %step_hbm.1, s32[8,128]{1,0:T(8,128)} %bitcast.4, s32[1,128]{1,0:T(1,128)} %tile_frame_hbm.1, s32[1,128]{1,0:T(1,128)} %tile_step_hbm.1, s32[1,1]{1,0:T(1,128)} %bitcast.3.count_hbm, ...), custom_call_target="tpu_custom_call" | custom-call | tf_op jit(solution)/shard_map/contrastive/pallas_call | solution.py:373
  48.8 1.4 %hand_over.1 = (f32[8,128]{1,0:T(8,128)}, bf16[1024,1024]{1,0:T(8,128)(2,1)}, f32[128,512]{1,0:T(8,128)}) custom-call(f32[8,128]{1,0:T(8,128)S(1)} %get-tuple-element.9.loss, bf16[1024,1024]{1,0:T(8,128)(2,1)S(1)} %get-tuple-element.10.grad, f32[128,512]{1,0:T(8,128)S(1)} %get-tuple-element.11.step_grad), custom_call_target="tpu_custom_call" | custom-call | tf_op jit(solution)/shard_map/hand_over/pallas_call | solution.py:423

commit v5 on v4

--- a/solution.py
+++ b/solution.py
@@ -26,7 +26,7 @@
 POS = {place: k for k, place in enumerate(ORDER)}
 TURN = [POS[(db, da)] for da, db in ORDER]
 
-GATHER = {1: [(3, 0), (1, 0), (0, 3), (0, 1)], 2: [(2, 0)], 3: [(3, 3), (3, 1)], 4: [(1, 1), (1, 3)], 5: [(2, 1), (2, 3)], 7: [(0, 2)], 8: [(3, 2), (1, 2)], 11: [(2, 2)]}
+GATHER = {1: [(3, 0), (1, 0), (0, 3), (0, 1)], 2: [(2, 0)], 3: [(3, 3), (3, 1)], 4: [(1, 1), (1, 3)], 5: [(2, 1), (2, 3)], 7: [(0, 2)], 8: [(3, 2), (1, 2)], 12: [(2, 2)]}
 ONWARD = {
     (0, 0): ['a+', 'a-', 'b+', 'b-', 'a2'],
     (3, 0): ["b+", "b-"],
@@ -71,7 +71,7 @@
 REDUCE_LATE = {(0, 0): [(0, 3)], (0, 1): [(0, 1), (2, 0)], (1, 0): [(3, 0), (1, 0)]}
 EARLY = 4
 LATE = CHIPS - EARLY
-GROUP = 1
+PAIRED = 8
 
 
 def kernel(
@@ -190,24 +190,25 @@
         ).astype(BF16)
         emb_t[:, rows] = emb[rows, :].T
 
-    def score(k, early):
+    def score(k, first, last, group):
+        early = last <= EARLY
         for step in GATHER:
-            if (step * GROUP < EARLY) == early:
-                @pl.when(k == step)
+            if first <= step < last:
+                @pl.when(k * group == step)
                 def _():
                     for place in GATHER[step]:
                         arrive(place)
         tabs, turns = [], []
-        for g in range(GROUP):
-            j = k * GROUP + g
+        for g in range(group):
+            j = k * group + g
             remote(others(j), others(j), ag_send.at[0], ag_other.at[j], "side").wait_recv()
             tabs.append(table[j])
             turns.append(tabs[-1].T)
         tab = jnp.concatenate(tabs, axis=0)
         turned = jnp.concatenate(turns, axis=1)
-        tall = 2 * BLK * GROUP
+        tall = 2 * BLK * group
         if not early:
-            base = pl.multiple_of((k * GROUP - EARLY) * 2 * BLK, tall)
+            base = pl.multiple_of((k * group - EARLY) * 2 * BLK, tall)
             table_t[:, pl.ds(base, tall)] = turned
         for n in range(pieces):
             fs = slice(n * cols, (n + 1) * cols)
@@ -215,17 +216,17 @@
             parts = []
             before = top[:, fs]
             after = before
-            for g in range(2 * GROUP):
+            for g in range(2 * group):
                 j, h = g // 2, g % 2
                 value = raw[g * BLK : (g + 1) * BLK] * (temper * LOG2E) + bias[
-                    k * GROUP + j, h : h + 1, fs
+                    k * group + j, h : h + 1, fs
                 ]
-                scores[k * GROUP + j, h * BLK : (h + 1) * BLK, fs] = value
+                scores[k * group + j, h * BLK : (h + 1) * BLK, fs] = value
                 after = jnp.maximum(after, jnp.max(value, axis=0, keepdims=True))
                 parts.append(value)
             fade = jnp.exp2(before - after)
             gained = total[:, fs] * fade
-            for g in range(2 * GROUP):
+            for g in range(2 * group):
                 value = jnp.exp2(parts[g] - after)
                 gained = gained + jnp.sum(value, axis=0, keepdims=True)
                 if early:
@@ -237,15 +238,19 @@
                     turned, near[:, fs], preferred_element_type=F32
                 )
 
-    @pl.loop(0, EARLY // GROUP)
+    @pl.loop(0, EARLY)
     def _(k):
-        score(k, True)
+        score(k, 0, EARLY, 1)
 
     shift[...] = top[...]
 
-    @pl.loop(EARLY // GROUP, CHIPS // GROUP)
+    @pl.loop(EARLY, PAIRED)
     def _(k):
-        score(k, False)
+        score(k, EARLY, PAIRED, 1)
+
+    @pl.loop(PAIRED // 2, CHIPS // 2)
+    def _(k):
+        score(k, PAIRED, CHIPS, 2)
 
     lse = top[...] + jnp.log(total[...]) * LOG2E
     top[...] = jnp.exp2(shift[...] - lse)
@@ -385,7 +390,7 @@
             pltpu.VMEM((width, BLK), BF16),
             pltpu.VMEM((CHIPS, 2 * BLK, n_frames), F32),
             pltpu.VMEM((CHIPS * 2 * BLK, n_frames), BF16),
-            pltpu.VMEM((GROUP * 2 * BLK, n_frames), BF16),
+            pltpu.VMEM((2 * BLK, n_frames), BF16),
             pltpu.VMEM((width, n_frames), F32),
             pltpu.VMEM((CHIPS, 2, n_frames), F32),
             pltpu.VMEM((1, n_frames), F32),

time: 50.3 us -> 50.4 us (level)
  no operation moved by 1% of the time
where the time goes in v5:
time: 50.4 us; the launch traced here: 50.3 us
  Pallas kernels  49 us (97%)
  between operations  1.29 us (3%)
    pallas_call x1, Pallas kernels, shards(): pl.pallas_call(kernel, name='contrastive', out_shape=held, in_specs=[anyw...  47.6 us
    pallas_call x1, Pallas kernels, shards(): pl.pallas_call(hand_over, name='hand_over', out_shape=results, in_specs=[...  1.42 us

profile of v5, /device:TPU:1, one launch (start us, length us, event | category | flops | bytes accessed | tf_op | source)
XLA Modules:
  0.0 50.3 jit_solution(17116790947187097200)
XLA Ops:
  1.3 47.6 %contrastive.1 = (f32[8,128]{1,0:T(8,128)S(1)}, bf16[1024,1024]{1,0:T(8,128)(2,1)S(1)}, f32[128,512]{1,0:T(8,128)S(1)}) custom-call(bf16[128,512]{1,0:T(8,128)(2,1)} %step_hbm.1, s32[8,128]{1,0:T(8,128)} %bitcast.4, s32[1,128]{1,0:T(1,128)} %tile_frame_hbm.1, s32[1,128]{1,0:T(1,128)} %tile_step_hbm.1, s32[1,1]{1,0:T(1,128)} %bitcast.3.count_hbm, ...), custom_call_target="tpu_custom_call" | custom-call | tf_op jit(solution)/shard_map/contrastive/pallas_call | solution.py:378
  48.9 1.4 %hand_over.1 = (f32[8,128]{1,0:T(8,128)}, bf16[1024,1024]{1,0:T(8,128)(2,1)}, f32[128,512]{1,0:T(8,128)}) custom-call(f32[8,128]{1,0:T(8,128)S(1)} %get-tuple-element.9.loss, bf16[1024,1024]{1,0:T(8,128)(2,1)S(1)} %get-tuple-element.10.grad, f32[128,512]{1,0:T(8,128)S(1)} %get-tuple-element.11.step_grad), custom_call_target="tpu_custom_call" | custom-call | tf_op jit(solution)/shard_map/hand_over/pallas_call | solution.py:428
